TPU v7x, 32 devices: a whole 2x2x4 slice. The times are simulated.
32 devices in a mesh: groups: 2 (over y), cand: 4 (over z), tensor: 4 (over x, core).
Axes of the slice: x: 2, y: 2, z: 4, core: 2. Of those that a mesh axis runs over, the one named last changes fastest.
Arguments:
- response_latest_embeddings: bfloat16 [16, 384, 8192], P(('groups', 'cand'), None, 'tensor'), parts along dimension 0, may hold values from -6 to 6
- critic_probe_projector: bfloat16 [8192, 4096], P('cand', 'tensor'), may hold values from -0.0625 to 0.0625
- critic_pair_projector: bfloat16 [8192, 2048], P('cand', 'tensor'), may hold values from -0.0625 to 0.0625
- critic_stored_pairs: bfloat16 [16, 2048, 2048], P(('groups', 'cand'), None, 'tensor'), parts along dimension 0, may hold values from -1000 to 1000
- critic_grading_vector: float32 [4096], P('tensor'), may hold values from -6 to 6
- actor_stored_pairs: bfloat16 [16, 2048, 8, 256], P(('groups', 'cand'), None, 'tensor'), parts along dimension 0, may hold values from -1000 to 1000
- filled_extents: int32 [16], P('groups'), parts along dimension 0, may hold values from 1 to 2048, as said below
- kept_responses: int32 [8], P('groups'), parts along dimension 0, may hold values from 0 to 7, as said below
- actor_latest_probes: bfloat16 [8, 4, 4096], P(('groups', 'cand'), None, 'tensor'), parts along dimension 0, may hold values from -6 to 6
- actor_latest_pairs: bfloat16 [8, 4, 2048], P(('groups', 'cand'), None, 'tensor'), parts along dimension 0, may hold values from -6 to 6
Outputs:
- token_rewards: float32 [16, 384], P(('groups', 'cand')), parts along dimension 0
- actor_mixing_result: bfloat16 [8, 4, 4096], P(('groups', 'cand'), None, 'tensor'), parts along dimension 0
There are 2 independent parts, one for each index of `groups`. A program takes and returns all parts, laid end to end along the dimension named above; an argument that names none is the same for every part. Nothing has to cross between parts.
Inputs may be any that keep to these rules, and one draw needn't show every extreme that they name: `kept_responses`: distinct candidate ids, always including 0 and 7. `filled_extents`: some candidate has exactly 2048 live tokens.
All inputs are finite; a program needn't handle non-finite values.
Results may differ from a plain program's by a relative error of at most 0.012.
The roundings to bfloat16 on the way count: a program that leaves them out, or rounds other values in their place, can miss the bound.
Values may be sent and summed in bfloat16 or wider, within the bound.
A program may use at most 128 MiB of HBM per device.

v0:
```python
import jax
import jax.numpy as jnp
from jax import lax
from jax.sharding import PartitionSpec as P

HD = 128


masked_value = -1e30


def local(
    response_latest_embeddings,
    critic_probe_projector,
    critic_pair_projector,
    critic_stored_pairs,
    critic_grading_vector,
    actor_stored_pairs,
    filled_extents,
    kept_responses,
    actor_latest_probes,
    actor_latest_pairs,
):
    cand_here = response_latest_embeddings.shape[0]
    span_len = response_latest_embeddings.shape[1]
    key_scale = HD ** (-0.5)
    whole_states = lax.all_gather(response_latest_embeddings, "tensor", axis=2, tiled=True)
    full_width = whole_states.shape[2]
    tok_rows = whole_states.reshape(cand_here * span_len, full_width)
    query_cols = critic_probe_projector.shape[1]
    keyval_cols = critic_pair_projector.shape[1]
    query_sum = jnp.dot(
        tok_rows,
        lax.all_gather(critic_probe_projector, "cand", axis=0, tiled=True),
        preferred_element_type=jnp.float32,
    )
    keyval_sum = jnp.dot(
        tok_rows,
        lax.all_gather(critic_pair_projector, "cand", axis=0, tiled=True),
        preferred_element_type=jnp.float32,
    )
    heads_here = query_cols // HD
    groups_here = keyval_cols // (2 * HD)
    per_group = heads_here // groups_here
    query_heads = query_sum.astype(jnp.bfloat16).reshape(
        cand_here, span_len, groups_here, per_group, HD
    )
    keyval = keyval_sum.astype(jnp.bfloat16).reshape(cand_here, span_len, groups_here, 2 * HD)
    context = critic_stored_pairs.shape[1]
    cached = critic_stored_pairs.reshape(cand_here, context, groups_here, 2 * HD)
    every_key = jnp.concatenate([cached, keyval], axis=1)
    causal = lax.broadcasted_iota(jnp.int32, (span_len, span_len), 0) >= lax.broadcasted_iota(
        jnp.int32, (span_len, span_len), 1
    )
    visible = jnp.concatenate([jnp.ones((span_len, context), dtype=bool), causal], axis=1)

    def score_one(entry_pair):
        queries, keys_values = entry_pair
        scores = (
            jnp.einsum(
                "tkgd,skd->kgts", queries, keys_values[..., :HD], preferred_element_type=jnp.float32
            )
            * key_scale
        )
        scores = jnp.where(visible, scores, masked_value)
        rounded = jax.nn.softmax(scores, axis=-1).astype(jnp.bfloat16)
        heads_out = jnp.einsum(
            "kgts,skd->tkgd", rounded, keys_values[..., HD:], preferred_element_type=jnp.float32
        )
        return jnp.dot(
            heads_out.reshape(span_len, heads_here * HD),
            critic_grading_vector,
            precision=lax.Precision.HIGHEST,
        )

    partial_reward = lax.map(score_one, (query_heads, every_key))
    token_rewards = lax.psum(partial_reward, "tensor")
    device_here = lax.axis_index("cand")
    lane_number = kept_responses.shape[0]
    new_count = actor_latest_probes.shape[1]
    kv_here = actor_stored_pairs.shape[2]
    policy_heads = actor_latest_probes.shape[2] // HD
    policy_group = policy_heads // kv_here
    cache_len = actor_stored_pairs.shape[1]
    causal_new = lax.broadcasted_iota(jnp.int32, (new_count, new_count), 0) >= lax.broadcasted_iota(
        jnp.int32, (new_count, new_count), 1
    )
    all_queries, all_fresh = (
        lax.all_gather(actor_latest_probes, "cand", axis=0, tiled=True),
        lax.all_gather(actor_latest_pairs, "cand", axis=0, tiled=True),
    )
    ids_here = device_here * cand_here + lax.broadcasted_iota(jnp.int32, (cand_here,), 0)
    matched = kept_responses[None, :] == ids_here[:, None]
    slot_index = jnp.sum(
        jnp.where(matched, lax.broadcasted_iota(jnp.int32, (cand_here, lane_number), 1), 0), axis=1
    )
    own_queries = jnp.take(all_queries, slot_index, axis=0).reshape(
        cand_here, new_count, kv_here, policy_group, HD
    )
    own_fresh = jnp.take(all_fresh, slot_index, axis=0).reshape(
        cand_here, new_count, kv_here, 2 * HD
    )
    sequence_places = lax.broadcasted_iota(jnp.int32, (cache_len,), 0)
    living_response_flags = sequence_places[None, :] < jnp.take(filled_extents, ids_here)[:, None]
    living_response_flags = living_response_flags[:, None, None, None, :]
    scores = (
        jnp.einsum(
            "cikgd,ctkd->ckgit",
            own_queries,
            actor_stored_pairs[..., :HD],
            preferred_element_type=jnp.float32,
        )
        * key_scale
    )
    scores = jnp.where(living_response_flags, scores, masked_value)
    fresh_scores = (
        jnp.einsum(
            "cikgd,cjkd->ckgij",
            own_queries,
            own_fresh[..., :HD],
            preferred_element_type=jnp.float32,
        )
        * key_scale
    )
    fresh_scores = jnp.where(causal_new, fresh_scores, masked_value)
    peak_score = jnp.maximum(jnp.max(scores, axis=-1), jnp.max(fresh_scores, axis=-1))
    old_weights = jnp.where(living_response_flags, jnp.exp(scores - peak_score[..., None]), 0.0)
    fresh_weights = jnp.where(causal_new, jnp.exp(fresh_scores - peak_score[..., None]), 0.0)
    denominator = jnp.sum(old_weights, axis=-1) + jnp.sum(fresh_weights, axis=-1)
    numerator = jnp.einsum(
        "ckgit,ctkd->ckgid",
        old_weights,
        actor_stored_pairs[..., HD:],
        preferred_element_type=jnp.float32,
    )
    numerator = numerator + jnp.einsum(
        "ckgij,cjkd->ckgid", fresh_weights, own_fresh[..., HD:], preferred_element_type=jnp.float32
    )
    result = numerator / denominator[..., None]
    flattened = jnp.transpose(result, (0, 3, 1, 2, 4)).reshape(
        cand_here, new_count * policy_heads * HD
    )
    placed = jnp.einsum(
        "cs,cx->sx", matched.astype(jnp.float32), flattened, precision=lax.Precision.HIGHEST
    )
    slot_rows = lax.psum_scatter(
        placed.reshape(lane_number, new_count, policy_heads * HD).astype(jnp.bfloat16),
        "cand",
        scatter_dimension=0,
        tiled=True,
    )
    return (token_rewards, slot_rows)


def solution(mesh):
    placed = (
        P(("groups", "cand"), None, "tensor"),
        P("cand", "tensor"),
        P("cand", "tensor"),
        P(("groups", "cand"), None, "tensor"),
        P("tensor"),
        P(("groups", "cand"), None, "tensor", None),
        P("groups"),
        P("groups"),
        P(("groups", "cand"), None, "tensor"),
        P(("groups", "cand"), None, "tensor"),
    )
    return jax.shard_map(
        local,
        mesh=mesh,
        in_specs=placed,
        out_specs=(P(("groups", "cand"), None), P(("groups", "cand"), None, "tensor")),
        check_vma=False,
    )
```

profile of v0, /device:TPU:0, one launch (start us, length us, event | category | flops | bytes accessed | tf_op | source)
XLA Modules:
  0.0 638.4 jit_solution(14081413601439974650)
XLA Ops:
  7.2 0.7 all-gather.6.cloned.1.call-update
  8.0 0.7 all-gather.4.cloned.1.call-update
  8.7 0.7 all-gather.8.cloned.1.call-update
  9.5 6.3 copy.40
  15.8 0.6 gather_fusion
  16.4 15.2 %all_gather.18 = bf16[4,4,1024]{2,1,0:T(4,128)(2,1)S(1)} all-gather(bf16[1,4,1024]{2,1,0:T(4,128)(2,1)S(1)} %copy-done.4), channel_id=1, replica_groups=mesh['groups'=2,'cand'=4,'tensor'=4] {'cand'}, dimensions={0}, use_global_device_ids=true | all-gather | bytes 40960 | tf_op jit(solution)/shard_map/all_gather | solution.py:89
  31.7 0.2 fusion.26
  31.9 0.6 gather_fusion.1
  32.5 19.5 %all_gather.19 = bf16[4,4,512]{2,1,0:T(4,128)(2,1)S(1)} all-gather(bf16[1,4,512]{2,1,0:T(4,128)(2,1)S(1)} %copy-done.5), channel_id=1, replica_groups=mesh['groups'=2,'cand'=4,'tensor'=4] {'cand'}, dimensions={0}, use_global_device_ids=true | all-gather | bytes 20480 | tf_op jit(solution)/shard_map/all_gather | solution.py:90
  51.9 0.6 gather_fusion.2
  52.5 0.1 broadcast_select_fusion
  52.6 0.3 fusion.36
  53.0 0.1 iota_compare_fusion.1
  53.0 4.7 fusion.34
  57.8 0.8 fusion.35
  58.6 0.1 fusion.22
  58.7 0.4 fusion.18
  59.1 0.6 fusion.13
  59.7 0.3 fusion.15
  60.0 0.3 convolution_convert_fusion.2
  60.4 1.2 concatenate.7
  61.6 0.6 dynamic-slice
  62.2 24.7 %all-reduce.1 = bf16[4,4,1024]{2,1,0:T(4,128)(2,1)S(1)} all-reduce(bf16[4,4,1024]{2,1,0:T(4,128)(2,1)S(1)} %copy.52), channel_id=2, replica_groups=mesh['groups'=2,'cand'=4,'tensor'=4] {'cand'}, use_global_device_ids=true, to_apply=%region_10.11.clone | all-reduce | flops 16384 | bytes 65536
  86.9 1.2 constant_dynamic-slice_fusion.2
  88.1 75.4 %all-gather.6.cloned.1.call-done = bf16[8192,512]{1,0:T(8,128)(2,1)} async-done(((bf16[2048,512]{1,0:T(8,128)(2,1)}), bf16[8192,512]{1,0:T(8,128)(2,1)}) %all-gather.6.cloned.1.call-update) | async-done | bytes 8388624 | tf_op jit(solution)/shard_map/all_gather | solution.py:39
  163.5 81.9 %all-gather.4.cloned.1.call-done = bf16[2,384,8192]{2,1,0:T(8,128)(2,1)} async-done(((bf16[2,384,2048]{2,1,0:T(8,128)(2,1)}), bf16[2,384,8192]{2,1,0:T(8,128)(2,1)}) %all-gather.4.cloned.1.call-update) | async-done | bytes 12582928 | tf_op jit(solution)/shard_map/all_gather | solution.py:27
  245.4 12.0 %convolution_convert_fusion.1 = bf16[768,512]{1,0:T(8,128)(2,1)S(1)} fusion(bf16[768,8192]{1,0:T(8,128)(2,1)} %bitcast.129, bf16[8192,512]{1,0:T(8,128)(2,1)} %all-gather.6.cloned.1.call-done), kind=kOutput, calls=%fused_computation.29 | convolution fusion | flops 6442844160 | bytes 21757952 | tf_op jit(solution)/shard_map/dot_general | solution.py:37
  257.4 0.2 reshape.109
  257.6 0.6 copy.41
  258.2 5.4 pad_maximum_fusion
  263.7 270.1 %all-gather.8.cloned.1.call-done = bf16[8192,1024]{1,0:T(8,128)(2,1)} async-done(((bf16[2048,1024]{1,0:T(8,128)(2,1)}), bf16[8192,1024]{1,0:T(8,128)(2,1)}) %all-gather.8.cloned.1.call-update) | async-done | bytes 16777232 | tf_op jit(solution)/shard_map/all_gather | solution.py:34
  533.7 18.7 %convolution_convert_fusion = bf16[768,1024]{1,0:T(8,128)(2,1)S(1)} fusion(bf16[768,8192]{1,0:T(8,128)(2,1)} %bitcast.130, bf16[8192,1024]{1,0:T(8,128)(2,1)} %all-gather.8.cloned.1.call-done), kind=kOutput, calls=%fused_computation.28 | convolution fusion | flops 12885688320 | bytes 30932992 | tf_op jit(solution)/shard_map/dot_general | solution.py:32
  552.5 2.4 reshape.110
  554.9 69.6 %while.10 = (s32[]{:T(128)}, f32[2,384]{1,0:T(2,128)S(1)}, bf16[2,2432,2,256]{1,3,2,0:T(8,128)(2,1)}, pred[384,2432]{0,1:T(8,128)(4,1)}, bf16[2,384,2,4,128]{4,3...) while((s32[]{:T(128)}, f32[2,384]{1,0:T(2,128)S(1)}, bf16[2,2432,2,256]{1,3,2,0:T(8,128)(2,1)}, ...), condition=%wide.region_3.4_spmd, body=%wide.region_0.3_spmd.sunk | while | flops 3874753024 | bytes 88654472 | solution.py:76
  554.9 1.9 constant_dynamic-slice_fusion.5
  556.7 2.6 copy.94
  559.4 1.4 constant_dynamic-slice_fusion.6
  560.8 17.0 %fusion.52 = (f32[2,4,384]{2,1,0:T(4,128)S(1)}, f32[2,4,384,2432]{2,3,1,0:T(8,128)}) fusion(pred[384,2432]{0,1:T(8,128)(4,1)} %get-tuple-element.139, bf16[2432,2,256]{2,0,1:T(8,128)(2,1)} %bitcast.122, bf16[1,384,2,4,128]{4,3,2,1,0:T(4,128)(2,1)S(1)} %constant_dynamic-slice_fusion.6), kind=kOutput, calls=%fused_computation.74.clone.1 | convolution fusion | flops 1942489472 | bytes 32862208 | tf_op jit(solution)/shard_map/while/body/eval_jaxpr/sub | solution.py:66
  577.8 10.9 %fusion.53 = f32[2,128,4,384]{3,1,2,0:T(8,128)S(1)} fusion(f32[2,4,384,2432]{2,3,1,0:T(8,128)} %get-tuple-element.118, f32[2,4,384]{2,1,0:T(4,128)S(1)} %get-tuple-element.119, bf16[2432,2,256]{2,0,1:T(8,128)(2,1)S(1)} %bitcast.123), kind=kOutput, calls=%fused_computation.11.clone.1 | convolution fusion | flops 1927544832 | bytes 32714752 | tf_op jit(solution)/shard_map/while/body/eval_jaxpr/kgts,skd->tkgd/dot_general | solution.py:67
  588.7 0.9 fusion.54
  589.6 0.1 dynamic_update_slice.5
  589.7 1.9 constant_dynamic-slice_fusion.5
  591.6 2.6 copy.94
  594.2 1.4 constant_dynamic-slice_fusion.6
  595.6 17.0 %fusion.52 = (f32[2,4,384]{2,1,0:T(4,128)S(1)}, f32[2,4,384,2432]{2,3,1,0:T(8,128)}) fusion(pred[384,2432]{0,1:T(8,128)(4,1)} %get-tuple-element.139, bf16[2432,2,256]{2,0,1:T(8,128)(2,1)} %bitcast.122, bf16[1,384,2,4,128]{4,3,2,1,0:T(4,128)(2,1)S(1)} %constant_dynamic-slice_fusion.6), kind=kOutput, calls=%fused_computation.74.clone.1 | convolution fusion | flops 1942489472 | bytes 32862208 | tf_op jit(solution)/shard_map/while/body/eval_jaxpr/sub | solution.py:66
  612.6 10.9 %fusion.53 = f32[2,128,4,384]{3,1,2,0:T(8,128)S(1)} fusion(f32[2,4,384,2432]{2,3,1,0:T(8,128)} %get-tuple-element.118, f32[2,4,384]{2,1,0:T(4,128)S(1)} %get-tuple-element.119, bf16[2432,2,256]{2,0,1:T(8,128)(2,1)S(1)} %bitcast.123), kind=kOutput, calls=%fused_computation.11.clone.1 | convolution fusion | flops 1927544832 | bytes 32714752 | tf_op jit(solution)/shard_map/while/body/eval_jaxpr/kgts,skd->tkgd/dot_general | solution.py:67
  623.5 0.9 fusion.54
  624.5 7.4 %psum.7 = f32[2,384]{1,0:T(2,128)} all-reduce(f32[2,384]{1,0:T(2,128)S(1)} %get-tuple-element.34), channel_id=1, replica_groups=mesh['groups'=2,'cand'=4,'tensor'=4] {'tensor'}, use_global_device_ids=true, to_apply=%region_4.5 | all-reduce | flops 768 | bytes 6144 | tf_op jit(solution)/shard_map/psum | solution.py:77
  (37 shorter events, 0.4 us)
Async XLA Ops:
  7.2 8.6 %copy-start = (s32[8]{0:T(128)S(1)}, s32[8]{0:T(128)}, u32[]{:S(2)}) copy-start(s32[8]{0:T(128)} %param.18) | copy-start | bytes 100
  7.2 156.3 %all-gather.6.cloned.1.call-start = ((), (), s32[]{:S(2)}) async-start(), calls=%async_computation.1 | async-start | bytes 10485760 | tf_op jit(solution)/shard_map/all_gather | solution.py:39
  7.9 237.4 %all-gather.4.cloned.1.call-start = ((), (), s32[]{:S(2)}) async-start(), calls=%async_computation | async-start | bytes 15728640 | tf_op jit(solution)/shard_map/all_gather | solution.py:27
  8.7 525.1 %all-gather.8.cloned.1.call-start = ((), (), s32[]{:S(2)}) async-start(), calls=%async_computation.2 | async-start | bytes 20971520 | tf_op jit(solution)/shard_map/all_gather | solution.py:34
  9.4 7.0 %copy-start.4 = (bf16[1,4,1024]{2,1,0:T(4,128)(2,1)S(1)}, bf16[1,4,1024]{2,1,0:T(4,128)(2,1)}, u32[]{:S(2)}) copy-start(bf16[1,4,1024]{2,1,0:T(4,128)(2,1)} %param.20) | copy-start | bytes 24580
  9.4 22.2 %copy-start.6 = (s32[4]{0:T(128)S(1)}, s32[4]{0:T(128)}, u32[]{:S(2)}) copy-start(s32[4]{0:T(128)} %param.19) | copy-start | bytes 52
  9.4 23.0 %copy-start.5 = (bf16[1,4,512]{2,1,0:T(4,128)(2,1)S(1)}, bf16[1,4,512]{2,1,0:T(4,128)(2,1)}, u32[]{:S(2)}) copy-start(bf16[1,4,512]{2,1,0:T(4,128)(2,1)} %param.21) | copy-start | bytes 12292
  57.8 3.8 copy-start.7
  263.7 291.2 %copy-start.3 = (f32[1024]{0:T(1024)S(1)}, f32[1024]{0:T(1024)}, u32[]{:S(2)}) copy-start(f32[1024]{0:T(1024)} %param.16) | copy-start | bytes 12292
  560.8 17.0 %copy-start.2 = (bf16[1,2432,2,256]{3,1,2,0:T(8,128)(2,1)S(1)}, bf16[1,2432,2,256]{3,1,2,0:T(8,128)(2,1)}, u32[]{:S(2)}) copy-start(bf16[1,2432,2,256]{3,1,2,0:T(8,128)(2,1)} %copy.94) | copy-start | bytes 7471108 | tf_op jit(solution)/shard_map/while
  595.6 17.0 %copy-start.2 = (bf16[1,2432,2,256]{3,1,2,0:T(8,128)(2,1)S(1)}, bf16[1,2432,2,256]{3,1,2,0:T(8,128)(2,1)}, u32[]{:S(2)}) copy-start(bf16[1,2432,2,256]{3,1,2,0:T(8,128)(2,1)} %copy.94) | copy-start | bytes 7471108 | tf_op jit(solution)/shard_map/while
  624.5 7.4 %copy-start.1 = (s32[8]{0:T(128)S(1)}, s32[8]{0:T(128)}, u32[]{:S(2)}) copy-start(s32[8]{0:T(128)} %param.18) | copy-start | bytes 100
Sparse Core Ops, SparseCore 0:
  9.6 153.8 all-gather.5
  165.0 80.3 all-gather.3
  246.9 286.7 all-gather.7
where the time goes:
time: 639 us; the launch traced here: 638 us
  waiting for transfers between devices  429 us (67%)
  matrix products  90.7 us (14%)
  blocking collectives  66.8 us (10%)
  local copies, waits for them, and re-layouts  31 us (5%)
  between operations  14 us (2%)
    all_gather x1, waiting for transfers between devices, local(): lax.all_gather(critic_probe_projector, 'cand', axis=0, tiled=True)  270 us
    all_gather x1, waiting for transfers between devices, local(): lax.all_gather(response_latest_embeddings, 'tensor', axis=2, tiled=True)  81.9 us
    all_gather x1, waiting for transfers between devices, local(): lax.all_gather(critic_pair_projector, 'cand', axis=0, tiled=True)  75.4 us
    sub x2, matrix products, score_one(): rounded = jax.nn.softmax(scores, axis=-1).astype(jnp.bfloat16)  34 us
    unnamed x1, blocking collectives  24.7 us
    dot_general x2, matrix products, score_one(): jnp.einsum('kgts,skd->tkgd', rounded, keys_values[..., HD:], preferred_el...  21.8 us
    all_gather x1, blocking collectives, local(): lax.all_gather(actor_latest_pairs, 'cand', axis=0, tiled=True)  19.5 us
    dot_general x1, matrix products, local(): jnp.dot(tok_rows, lax.all_gather(critic_probe_projector, 'cand', axis=0,...  18.7 us
  transfers between devices with their start and end apart: 3, of which 3 were waited for; matrix products, arithmetic and copies ran while one was open for 6% of the time, Pallas kernels for 0%

commit v1 on v0

v1 whole, which is shorter than its diff:
```python
import functools

import jax
import jax.numpy as jnp
from jax import lax
from jax.experimental import pallas as pl
from jax.experimental.pallas import tpu as pltpu
from jax.sharding import PartitionSpec as P

HD = 128
CW = 2 * HD
AHEAD = 2
MESH = pl.DeviceIdType.MESH

masked_value = -1e30


def project_kernel(
    nz, nt, per_group,
    x_ref, wq_ref, wkv_ref, cache_ref, grade_ref, out_ref,
    xbuf, wbuf, cbuf, acts,
    load_sem, right_sem, left_sem, line_sem, pair_send, pair_recv,
    x_right, x_left, x_line, x_pair_send, x_pair_recv,
):
    nchunk, depth, _ = wbuf.shape
    dz = depth // nz
    half = dz // 2
    nx = nt // 2
    cands, span, _ = out_ref.shape
    context = cbuf.shape[1]
    qchunks = per_group * HD // CW
    stride = 1 + qchunks
    y = lax.axis_index("groups")
    z = lax.axis_index("cand")
    t = lax.axis_index("tensor")
    x = t // 2
    c = t - 2 * x

    loads = []
    for k in range(nchunk):
        g, j = k // stride, k % stride
        if j == 0:
            src = wkv_ref.at[:, pl.ds(g * CW, CW)]
        else:
            src = wq_ref.at[:, pl.ds((g * qchunks + j - 1) * CW, CW)]
        loads.append(
            pltpu.make_async_copy(
                src, wbuf.at[k, pl.ds(pl.multiple_of(z * dz, dz), dz), :], load_sem.at[k]
            )
        )
    x_load = pltpu.make_async_copy(x_ref, xbuf.at[t], load_sem.at[nchunk])
    c_load = pltpu.make_async_copy(cache_ref, cbuf, load_sem.at[nchunk + 1])
    for k in range(min(AHEAD, nchunk)):
        loads[k].start()
    x_load.start()
    for k in range(min(AHEAD, nchunk), nchunk):
        loads[k].start()
    c_load.start()

    barrier = pltpu.get_barrier_semaphore()

    def greet(device):
        pl.semaphore_signal(barrier, inc=1, device_id=device, device_id_type=MESH)

    greet({"groups": 1 - y})
    greet({"tensor": 2 * x + 1 - c})

    @pl.when(z > 0)
    def _():
        greet({"cand": z - 1})

    @pl.when(z < nz - 1)
    def _():
        greet({"cand": z + 1})

    @pl.when(x > 0)
    def _():
        greet({"tensor": t - 2})

    @pl.when(x < nx - 1)
    def _():
        greet({"tensor": t + 2})

    ends = [z > 0, z < nz - 1, x > 0, x < nx - 1]
    pl.semaphore_wait(barrier, 2 + sum(e.astype(jnp.int32) for e in ends))

    def remote(ref, send, recv, device):
        return pltpu.make_async_remote_copy(
            src_ref=ref, dst_ref=ref, send_sem=send, recv_sem=recv,
            device_id=device, device_id_type=MESH,
        )

    def piece(k, o, side):
        return wbuf.at[k, pl.ds(pl.multiple_of(o * dz + side * half, half), half), :]

    def go_right(k, o):
        return remote(piece(k, o, y), right_sem.at[k, o], line_sem.at[k, o], {"cand": z + 1})

    def go_left(k, o):
        return remote(piece(k, o, y), left_sem.at[k, o], line_sem.at[k, o], {"cand": z - 1})

    def to_pair(k, o):
        return remote(piece(k, o, y), pair_send.at[k, o], pair_recv.at[k, o], {"groups": 1 - y})

    def from_pair(k, o):
        return remote(piece(k, o, 1 - y), pair_send.at[k, o], pair_recv.at[k, o], {"groups": 1 - y})

    def send_own(k):
        @pl.when(z < nz - 1)
        def _():
            go_right(k, z).start()

        @pl.when(z > 0)
        def _():
            go_left(k, z).start()

    def x_go_right(o):
        return remote(xbuf.at[2 * o + c], x_right.at[o], x_line.at[o], {"tensor": t + 2})

    def x_go_left(o):
        return remote(xbuf.at[2 * o + c], x_left.at[o], x_line.at[o], {"tensor": t - 2})

    def x_to_pair(o):
        return remote(xbuf.at[2 * o + c], x_pair_send.at[o], x_pair_recv.at[o], {"tensor": 2 * x + 1 - c})

    def x_from_pair(o):
        return remote(xbuf.at[2 * o + 1 - c], x_pair_send.at[o], x_pair_recv.at[o], {"tensor": 2 * x + 1 - c})

    for k in range(min(AHEAD, nchunk)):
        loads[k].wait()
        send_own(k)
    x_load.wait()

    @pl.when(x < nx - 1)
    def _():
        x_go_right(x).start()

    @pl.when(x > 0)
    def _():
        x_go_left(x).start()

    x_to_pair(x).start()
    for k in range(min(AHEAD, nchunk), nchunk):
        loads[k].wait()
    c_load.wait()
    out_ref[...] = jnp.zeros_like(out_ref)

    def finish_x():
        for d in range(1, nx):
            @pl.when(x - d >= 0)
            def _(d=d):
                x_go_right(x - d).wait_recv()
                x_to_pair(x - d).start()

                @pl.when(x < nx - 1)
                def _():
                    x_go_right(x - d).start()

            @pl.when(x + d < nx)
            def _(d=d):
                x_go_left(x + d).wait_recv()
                x_to_pair(x + d).start()

                @pl.when(x > 0)
                def _():
                    x_go_left(x + d).start()

        for o in range(nx):
            x_from_pair(o).wait_recv()

    def relay(k):
        def one(d, carry):
            @pl.when(z - d >= 0)
            def _():
                o = z - d
                go_right(k, o).wait_recv()

                @pl.when(z < nz - 1)
                def _():
                    go_right(k, o).start()

                to_pair(k, o).start()

            @pl.when(z + d < nz)
            def _():
                o = z + d
                go_left(k, o).wait_recv()

                @pl.when(z > 0)
                def _():
                    go_left(k, o).start()

                to_pair(k, o).start()

            return carry

        lax.fori_loop(1, nz, one, 0)

    rows = cands * span
    dx = depth // nt
    row_tile = rows // 3

    def attend(k):
        g = k // stride
        base = pl.multiple_of(g * CW, CW)
        kv_at = g * stride
        ri = lax.broadcasted_iota(jnp.int32, (span, span), 0)
        ci = lax.broadcasted_iota(jnp.int32, (span, span), 1)
        head0 = (g * qchunks + (k - kv_at) - 1) * 2

        def one(b, carry):
            at = pl.ds(pl.multiple_of(b * span, span), span)
            old_k = cbuf[b, :, pl.ds(base, HD)]
            old_v = cbuf[b, :, pl.ds(pl.multiple_of(base + HD, HD), HD)]
            new_k = acts[kv_at, at, :HD]
            new_v = acts[kv_at, at, HD:]
            for h in range(2):
                q = acts[k, at, h * HD:(h + 1) * HD]
                dims = (((1,), (1,)), ((), ()))
                s1 = lax.dot_general(q, old_k, dims, preferred_element_type=jnp.float32)
                s2 = lax.dot_general(q, new_k, dims, preferred_element_type=jnp.float32)
                s2 = jnp.where(ri >= ci, s2, masked_value)
                top = jnp.maximum(
                    jnp.max(s1, axis=1, keepdims=True), jnp.max(s2, axis=1, keepdims=True)
                )
                scale = HD ** -0.5
                e1 = jnp.exp((s1 - top) * scale)
                e2 = jnp.exp((s2 - top) * scale)
                total = jnp.sum(e1, axis=1, keepdims=True) + jnp.sum(e2, axis=1, keepdims=True)
                o = jnp.dot(e1.astype(jnp.bfloat16), old_v, preferred_element_type=jnp.float32)
                o = o + jnp.dot(e2.astype(jnp.bfloat16), new_v, preferred_element_type=jnp.float32)
                weight = grade_ref[pl.ds(head0 + h, 1), :]
                out_ref[b] += (o / total) * weight
            return carry

        lax.fori_loop(0, cands, one, 0)

    def compute(k):
        def take(d, carry):
            o = jnp.where(d < z, d, d + 1)
            from_pair(k, o).wait_recv()
            return carry

        lax.fori_loop(0, nz - 1, take, 0)

        def tile(r, carry):
            at = pl.ds(pl.multiple_of(r * row_tile, row_tile), row_tile)
            acc = jnp.zeros((row_tile, CW), jnp.float32)
            for s in range(nt):
                acc = acc + jnp.dot(
                    xbuf[s, at, :], wbuf[k, s * dx:(s + 1) * dx, :],
                    preferred_element_type=jnp.float32,
                )
            acts[k, at, :] = acc.astype(jnp.bfloat16)
            return carry

        lax.fori_loop(0, rows // row_tile, tile, 0)

        @pl.when(k % stride != 0)
        def _():
            attend(k)

    def done(k):
        return jnp.maximum(0, jnp.minimum(k, 2 * (k - 2)))

    def step(k, carry):
        @pl.when(k + AHEAD < nchunk)
        def _():
            send_own(k + AHEAD)

        relay(k)

        @pl.when(k == min(2, nchunk - 1))
        def _():
            finish_x()

        def inner(j, c2):
            compute(j)
            return c2

        last = jnp.where(k == nchunk - 1, nchunk, done(k))
        lax.fori_loop(done(k - 1), last, inner, 0)
        return carry

    lax.fori_loop(0, nchunk, step, 0)

    def drain(k, carry):
        def one(o, c2):
            @pl.when((o <= z) & (z < nz - 1))
            def _():
                go_right(k, o).wait_send()

            @pl.when((o >= z) & (z > 0))
            def _():
                go_left(k, o).wait_send()

            @pl.when(o != z)
            def _():
                to_pair(k, o).wait_send()

            return c2

        lax.fori_loop(0, nz, one, 0)
        return carry

    lax.fori_loop(0, nchunk, drain, 0)
    for o in range(nx):
        x_to_pair(o).wait_send()

        @pl.when((o <= x) & (x < nx - 1))
        def _(o=o):
            x_go_right(o).wait_send()

        @pl.when((o >= x) & (x > 0))
        def _(o=o):
            x_go_left(o).wait_send()


def reward_partial(nz, nt, x, wq, wkv, cache, grade):
    cands, span, dx = x.shape
    rows = cands * span
    depth = wq.shape[0] * nz
    groups_here = wkv.shape[1] // CW
    per_group = wq.shape[1] // HD // groups_here
    nchunk = (wq.shape[1] + wkv.shape[1]) // CW
    dma = pltpu.SemaphoreType.DMA
    nx = nt // 2
    anywhere = pl.BlockSpec(memory_space=pl.ANY)
    return pl.pallas_call(
        functools.partial(project_kernel, nz, nt, per_group),
        out_shape=jax.ShapeDtypeStruct((cands, span, HD), jnp.float32),
        in_specs=[anywhere] * 4 + [pl.BlockSpec(memory_space=pltpu.VMEM)],
        out_specs=pl.BlockSpec(memory_space=pltpu.VMEM),
        scratch_shapes=[
            pltpu.VMEM((nt, rows, dx), jnp.bfloat16),
            pltpu.VMEM((nchunk, depth, CW), jnp.bfloat16),
            pltpu.VMEM(cache.shape, jnp.bfloat16),
            pltpu.VMEM((nchunk, rows, CW), jnp.bfloat16),
            dma((nchunk + 2,)),
            dma((nchunk, nz)), dma((nchunk, nz)), dma((nchunk, nz)),
            dma((nchunk, nz)), dma((nchunk, nz)),
            dma((nx,)), dma((nx,)), dma((nx,)), dma((nx,)), dma((nx,)),
        ],
        compiler_params=pltpu.CompilerParams(
            collective_id=0, has_side_effects=True, vmem_limit_bytes=67043328
        ),
    )(x.reshape(rows, dx), wq, wkv, cache, grade.reshape(-1, HD))


def policy(
    cand_here, actor_stored_pairs, filled_extents, kept_responses, actor_latest_probes, actor_latest_pairs
):
    key_scale = HD ** (-0.5)
    device_here = lax.axis_index("cand")
    lane_number = kept_responses.shape[0]
    new_count = actor_latest_probes.shape[1]
    kv_here = actor_stored_pairs.shape[2]
    policy_heads = actor_latest_probes.shape[2] // HD
    policy_group = policy_heads // kv_here
    cache_len = actor_stored_pairs.shape[1]
    causal_new = lax.broadcasted_iota(jnp.int32, (new_count, new_count), 0) >= lax.broadcasted_iota(
        jnp.int32, (new_count, new_count), 1
    )
    both = lax.all_gather(
        jnp.concatenate([actor_latest_probes, actor_latest_pairs], axis=2), "cand", axis=0, tiled=True
    )
    all_queries = both[..., : policy_heads * HD]
    all_fresh = both[..., policy_heads * HD:]
    ids_here = device_here * cand_here + lax.broadcasted_iota(jnp.int32, (cand_here,), 0)
    matched = kept_responses[None, :] == ids_here[:, None]
    slot_index = jnp.sum(
        jnp.where(matched, lax.broadcasted_iota(jnp.int32, (cand_here, lane_number), 1), 0), axis=1
    )
    own_queries = jnp.take(all_queries, slot_index, axis=0).reshape(
        cand_here, new_count, kv_here, policy_group, HD
    )
    own_fresh = jnp.take(all_fresh, slot_index, axis=0).reshape(
        cand_here, new_count, kv_here, 2 * HD
    )
    sequence_places = lax.broadcasted_iota(jnp.int32, (cache_len,), 0)
    living = sequence_places[None, :] < jnp.take(filled_extents, ids_here)[:, None]
    living = living[:, None, None, None, :]
    scores = (
        jnp.einsum(
            "cikgd,ctkd->ckgit", own_queries, actor_stored_pairs[..., :HD],
            preferred_element_type=jnp.float32,
        )
        * key_scale
    )
    scores = jnp.where(living, scores, masked_value)
    fresh_scores = (
        jnp.einsum(
            "cikgd,cjkd->ckgij", own_queries, own_fresh[..., :HD], preferred_element_type=jnp.float32
        )
        * key_scale
    )
    fresh_scores = jnp.where(causal_new, fresh_scores, masked_value)
    peak = jnp.maximum(jnp.max(scores, axis=-1), jnp.max(fresh_scores, axis=-1))
    old_weights = jnp.where(living, jnp.exp(scores - peak[..., None]), 0.0)
    fresh_weights = jnp.where(causal_new, jnp.exp(fresh_scores - peak[..., None]), 0.0)
    denominator = jnp.sum(old_weights, axis=-1) + jnp.sum(fresh_weights, axis=-1)
    numerator = jnp.einsum(
        "ckgit,ctkd->ckgid", old_weights, actor_stored_pairs[..., HD:],
        preferred_element_type=jnp.float32,
    )
    numerator = numerator + jnp.einsum(
        "ckgij,cjkd->ckgid", fresh_weights, own_fresh[..., HD:], preferred_element_type=jnp.float32
    )
    result = numerator / denominator[..., None]
    flattened = jnp.transpose(result, (0, 3, 1, 2, 4)).reshape(
        cand_here, new_count * policy_heads * HD
    )
    placed = jnp.einsum(
        "cs,cx->sx", matched.astype(jnp.float32), flattened, precision=lax.Precision.HIGHEST
    )
    return lax.psum_scatter(
        placed.reshape(lane_number, new_count, policy_heads * HD).astype(jnp.bfloat16),
        "cand", scatter_dimension=0, tiled=True,
    )


def local(
    nz, nt,
    response_latest_embeddings,
    critic_probe_projector,
    critic_pair_projector,
    critic_stored_pairs,
    critic_grading_vector,
    actor_stored_pairs,
    filled_extents,
    kept_responses,
    actor_latest_probes,
    actor_latest_pairs,
):
    shares = reward_partial(
        nz, nt, response_latest_embeddings, critic_probe_projector, critic_pair_projector,
        critic_stored_pairs, critic_grading_vector,
    )
    token_rewards = lax.psum(jnp.sum(shares, axis=-1), "tensor")
    slot_rows = policy(
        response_latest_embeddings.shape[0], actor_stored_pairs, filled_extents, kept_responses,
        actor_latest_probes, actor_latest_pairs,
    )
    return (token_rewards, slot_rows)


def solution(mesh):
    placed = (
        P(("groups", "cand"), None, "tensor"),
        P("cand", "tensor"),
        P("cand", "tensor"),
        P(("groups", "cand"), None, "tensor"),
        P("tensor"),
        P(("groups", "cand"), None, "tensor", None),
        P("groups"),
        P("groups"),
        P(("groups", "cand"), None, "tensor"),
        P(("groups", "cand"), None, "tensor"),
    )
    return jax.shard_map(
        functools.partial(local, mesh.shape["cand"], mesh.shape["tensor"]),
        mesh=mesh,
        in_specs=placed,
        out_specs=(P(("groups", "cand"), None), P(("groups", "cand"), None, "tensor")),
        check_vma=False,
    )
```

time: 639 us -> 311 us (0.49)
  waiting for transfers between devices: 429 us -> 0 us
  Pallas kernels: 0 us -> 255 us
  matrix products: 90.7 us -> 2.35 us
  blocking collectives: 66.8 us -> 40.4 us
  local copies, waits for them, and re-layouts: 31 us -> 9.08 us
  between operations: 14 us -> 0.78 us
    all_gather x3 -> x0, waiting for transfers between devices: 427 us -> none  [the longest x1 270 us: local(): lax.all_gather(critic_probe_projector, 'cand', axis=0, tiled=True)]
    pallas_call x0 -> x1, Pallas kernels: none -> 255 us  [reward_partial(): pl.pallas_call(functools.partial(project_kernel, nz, nt, per_group), out_...]
    dot_general x11 -> x5, matrix products: 56.7 us -> 2.35 us  [the longest x1 0.81 us: policy(): jnp.einsum('cikgd,ctkd->ckgit', own_queries, actor_stored_pairs[..., :HD]...]
    sub x2 -> x0, matrix products: 34 us -> none  [score_one(): rounded = jax.nn.softmax(scores, axis=-1).astype(jnp.bfloat16)]
    all_gather x2 -> x1, blocking collectives: 34.7 us -> 14.8 us  [policy(): lax.all_gather(jnp.concatenate([actor_latest_probes, actor_latest_pairs],...]
    dynamic_slice x6 -> x0, local copies, waits for them, and re-layouts: 11.8 us -> none  [local(): partial_reward = lax.map(score_one, (query_heads, every_key))]
  transfers between devices with their start and end apart: 3 -> 0, of which waited for: 3 -> 0; matrix products, arithmetic and copies ran while one was open for 6% -> 0% of each run, Pallas kernels for 0% -> 0%
where the time goes in v1:
time: 311 us
  Pallas kernels  255 us (82%)
  blocking collectives  40.4 us (13%)
  local copies, waits for them, and re-layouts  9.08 us (3%)
  other arithmetic  3.45 us (1%)
    pallas_call x1, Pallas kernels, reward_partial(): pl.pallas_call(functools.partial(project_kernel, nz, nt, per_group), out_...  255 us
    unnamed x1, blocking collectives  19.2 us
    all_gather x1, blocking collectives, policy(): lax.all_gather(jnp.concatenate([actor_latest_probes, actor_latest_pairs],...  14.8 us
    psum x1, blocking collectives, local(): token_rewards = lax.psum(jnp.sum(shares, axis=-1), 'tensor')  6.42 us

profile of v1, /device:TPU:0, one launch (start us, length us, event | category | flops | bytes accessed | tf_op | source)
XLA Modules:
  0.0 310.6 jit_solution(17973546242401512797)
XLA Ops:
  0.7 1.3 gather_fusion
  2.0 0.8 fusion.15
  2.8 0.7 pad_maximum_fusion
  3.5 14.8 %all_gather.3 = bf16[4,4,1536]{2,1,0:T(4,128)(2,1)S(1)} all-gather(bf16[1,4,1536]{2,1,0:T(4,128)(2,1)S(1)} %pad_maximum_fusion), channel_id=1, replica_groups=mesh['groups'=2,'cand'=4,'tensor'=4] {'cand'}, dimensions={0}, use_global_device_ids=true | all-gather | bytes 61440 | tf_op jit(solution)/shard_map/all_gather | solution.py:364
  18.3 0.6 gather_fusion.2
  18.9 0.1 broadcast_select_fusion
  19.0 0.6 gather_fusion.1
  19.6 0.3 fusion.24
  20.0 0.1 iota_compare_fusion
  20.0 4.7 %fusion.22 = (bf16[2,2048,2,128]{3,2,1,0:T(2,128)(2,1)S(1)}, bf16[2,2048,2,128]{3,2,1,0:T(2,128)(2,1)S(1)}) fusion(bf16[2,2048,2,256]{3,2,1,0:T(2,128)(2,1)} %param.15), kind=kLoop, calls=%fused_computation.53 | loop fusion | bytes 8388608 | tf_op jit(solution)/shard_map/slice | solution.py:385
  24.7 0.8 fusion.23
  25.6 0.1 fusion.11
  25.7 0.0 copy-start
  25.7 0.4 fusion.7
  26.1 0.0 copy-start.1
  26.1 0.6 fusion.2
  26.7 0.3 fusion.4
  27.0 0.0 copy-done
  27.0 0.3 convolution_convert_fusion
  27.4 19.2 %all-reduce = bf16[4,4,1024]{2,1,0:T(4,128)(2,1)S(1)} all-reduce(bf16[4,4,1024]{2,1,0:T(4,128)(2,1)S(1)} %copy.36), channel_id=2, replica_groups=mesh['groups'=2,'cand'=4,'tensor'=4] {'cand'}, use_global_device_ids=true, to_apply=%region_7.8.clone | all-reduce | flops 16384 | bytes 65536
  46.6 0.0 copy-done.1
  46.6 0.6 dynamic-slice
  47.2 1.2 constant_dynamic-slice_fusion
  48.4 254.5 %shard_map.113 = f32[2,384,128]{2,1,0:T(8,128)} custom-call(bf16[768,2048]{1,0:T(8,128)(2,1)} %bitcast.53, bf16[2048,1024]{1,0:T(8,128)(2,1)} %wq_ref.1, bf16[2048,512]{1,0:T(8,128)(2,1)} %wkv_ref.1, bf16[2,2048,512]{2,1,0:T(8,128)(2,1)} %cache_ref.1, f32[8,128]{1,0:T(8,128)} %bitcast.56), custom_call_target="tpu_custom_call" | custom-call | tf_op jit(solution)/shard_map/pallas_call | solution.py:329
  303.0 1.2 reduce_sum.38
  304.1 6.4 %psum.7 = f32[2,384]{1,0:T(2,128)} all-reduce(f32[2,384]{1,0:T(2,128)S(1)} %reduce_sum.38), channel_id=1, replica_groups=mesh['groups'=2,'cand'=4,'tensor'=4] {'tensor'}, use_global_device_ids=true, to_apply=%region_1.0 | all-reduce | flops 768 | bytes 6144 | tf_op jit(solution)/shard_map/psum | solution.py:439
  (15 shorter events, 0.2 us)
Async XLA Ops:
  25.7 1.4 copy-start
  26.1 20.5 %copy-start.1 = (u32[32]{0:T(128)S(1)}, u32[32]{0:T(128)}, u32[]{:S(2)}) copy-start(u32[32]{0:T(128)} %constant.67) | copy-start | bytes 388

commit v2 on v1

--- a/solution.py
+++ b/solution.py
@@ -168,7 +168,7 @@
         for o in range(nx):
             x_from_pair(o).wait_recv()
 
-    def relay(k):
+    def relay(k, first, last):
         def one(d, carry):
             @pl.when(z - d >= 0)
             def _():
@@ -194,7 +194,7 @@
 
             return carry
 
-        lax.fori_loop(1, nz, one, 0)
+        lax.fori_loop(first, last, one, 0)
 
     rows = cands * span
     dx = depth // nt
@@ -256,21 +256,21 @@
 
         lax.fori_loop(0, rows // row_tile, tile, 0)
 
-        @pl.when(k % stride != 0)
+        @pl.when(lax.rem(k, stride) != 0)
         def _():
             attend(k)
 
     def done(k):
-        return jnp.maximum(0, jnp.minimum(k, 2 * (k - 2)))
+        return jnp.where(k < 2, 0, k)
 
     def step(k, carry):
         @pl.when(k + AHEAD < nchunk)
         def _():
             send_own(k + AHEAD)
 
-        relay(k)
-
-        @pl.when(k == min(2, nchunk - 1))
+        relay(k, 1, 2)
+
+        @pl.when(k == 2)
         def _():
             finish_x()
 
@@ -278,11 +278,12 @@
             compute(j)
             return c2
 
-        last = jnp.where(k == nchunk - 1, nchunk, done(k))
-        lax.fori_loop(done(k - 1), last, inner, 0)
+        lax.fori_loop(done(k - 1), done(k), inner, 0)
+        relay(k, 2, nz)
         return carry
 
     lax.fori_loop(0, nchunk, step, 0)
+    lax.fori_loop(nchunk - 1, nchunk, lambda j, c2: (compute(j), c2)[1], 0)
 
     def drain(k, carry):
         def one(o, c2):

time: 311 us -> 313 us (level)
  no operation moved by 1% of the time
where the time goes in v2:
time: 313 us; the launch traced here: 312 us
  Pallas kernels  256 us (82%)
  blocking collectives  40.2 us (13%)
  local copies, waits for them, and re-layouts  9.08 us (3%)
  other arithmetic  3.45 us (1%)
    pallas_call x1, Pallas kernels, reward_partial(): pl.pallas_call(functools.partial(project_kernel, nz, nt, per_group), out_...  256 us
    unnamed x1, blocking collectives  19.2 us
    all_gather x1, blocking collectives, policy(): lax.all_gather(jnp.concatenate([actor_latest_probes, actor_latest_pairs],...  14.8 us

profile of v2, /device:TPU:0, one launch (start us, length us, event | category | flops | bytes accessed | tf_op | source)
XLA Modules:
  0.0 312.3 jit_solution(6354253931588863351)
XLA Ops:
  0.7 1.3 gather_fusion
  2.0 0.8 fusion.15
  2.8 0.7 pad_maximum_fusion
  3.5 14.8 %all_gather.3 = bf16[4,4,1536]{2,1,0:T(4,128)(2,1)S(1)} all-gather(bf16[1,4,1536]{2,1,0:T(4,128)(2,1)S(1)} %pad_maximum_fusion), channel_id=1, replica_groups=mesh['groups'=2,'cand'=4,'tensor'=4] {'cand'}, dimensions={0}, use_global_device_ids=true | all-gather | bytes 61440 | tf_op jit(solution)/shard_map/all_gather | solution.py:365
  18.3 0.6 gather_fusion.2
  18.9 0.1 broadcast_select_fusion
  19.0 0.6 gather_fusion.1
  19.6 0.3 fusion.24
  20.0 0.1 iota_compare_fusion
  20.0 4.7 %fusion.22 = (bf16[2,2048,2,128]{3,2,1,0:T(2,128)(2,1)S(1)}, bf16[2,2048,2,128]{3,2,1,0:T(2,128)(2,1)S(1)}) fusion(bf16[2,2048,2,256]{3,2,1,0:T(2,128)(2,1)} %param.15), kind=kLoop, calls=%fused_computation.53 | loop fusion | bytes 8388608 | tf_op jit(solution)/shard_map/slice | solution.py:386
  24.7 0.8 fusion.23
  25.6 0.1 fusion.11
  25.7 0.0 copy-start
  25.7 0.4 fusion.7
  26.1 0.0 copy-start.1
  26.1 0.6 fusion.2
  26.7 0.3 fusion.4
  27.0 0.0 copy-done
  27.0 0.3 convolution_convert_fusion
  27.4 19.2 %all-reduce = bf16[4,4,1024]{2,1,0:T(4,128)(2,1)S(1)} all-reduce(bf16[4,4,1024]{2,1,0:T(4,128)(2,1)S(1)} %copy.36), channel_id=2, replica_groups=mesh['groups'=2,'cand'=4,'tensor'=4] {'cand'}, use_global_device_ids=true, to_apply=%region_7.8.clone | all-reduce | flops 16384 | bytes 65536
  46.6 0.0 copy-done.1
  46.6 0.6 dynamic-slice
  47.2 1.2 constant_dynamic-slice_fusion
  48.4 256.5 %shard_map.113 = f32[2,384,128]{2,1,0:T(8,128)} custom-call(bf16[768,2048]{1,0:T(8,128)(2,1)} %bitcast.53, bf16[2048,1024]{1,0:T(8,128)(2,1)} %wq_ref.1, bf16[2048,512]{1,0:T(8,128)(2,1)} %wkv_ref.1, bf16[2,2048,512]{2,1,0:T(8,128)(2,1)} %cache_ref.1, f32[8,128]{1,0:T(8,128)} %bitcast.56), custom_call_target="tpu_custom_call" | custom-call | tf_op jit(solution)/shard_map/pallas_call | solution.py:330
  304.9 1.2 reduce_sum.38
  306.1 6.2 %psum.7 = f32[2,384]{1,0:T(2,128)} all-reduce(f32[2,384]{1,0:T(2,128)S(1)} %reduce_sum.38), channel_id=1, replica_groups=mesh['groups'=2,'cand'=4,'tensor'=4] {'tensor'}, use_global_device_ids=true, to_apply=%region_1.0 | all-reduce | flops 768 | bytes 6144 | tf_op jit(solution)/shard_map/psum | solution.py:440
  (15 shorter events, 0.2 us)
Async XLA Ops:
  25.7 1.4 copy-start
  26.1 20.5 %copy-start.1 = (u32[32]{0:T(128)S(1)}, u32[32]{0:T(128)}, u32[]{:S(2)}) copy-start(u32[32]{0:T(128)} %constant.67) | copy-start | bytes 388

commit v3 on v2

--- a/solution.py
+++ b/solution.py
@@ -17,10 +17,11 @@
 
 def project_kernel(
     nz, nt, per_group,
-    x_ref, wq_ref, wkv_ref, cache_ref, grade_ref, out_ref,
+    x_ref, wq_ref, wkv_ref, cache_ref, grade_ref, slots_ref, out_ref, mine_ref,
     xbuf, wbuf, cbuf, acts,
     load_sem, right_sem, left_sem, line_sem, pair_send, pair_recv,
     x_right, x_left, x_line, x_pair_send, x_pair_recv,
+    given, give_send, give_recv,
 ):
     nchunk, depth, _ = wbuf.shape
     dz = depth // nz
@@ -65,13 +66,11 @@
     greet({"groups": 1 - y})
     greet({"tensor": 2 * x + 1 - c})
 
-    @pl.when(z > 0)
-    def _():
-        greet({"cand": z - 1})
-
-    @pl.when(z < nz - 1)
-    def _():
-        greet({"cand": z + 1})
+    def greet_peer(d, carry):
+        greet({"cand": lax.rem(z + d, nz)})
+        return carry
+
+    lax.fori_loop(1, nz, greet_peer, 0)
 
     @pl.when(x > 0)
     def _():
@@ -81,8 +80,8 @@
     def _():
         greet({"tensor": t + 2})
 
-    ends = [z > 0, z < nz - 1, x > 0, x < nx - 1]
-    pl.semaphore_wait(barrier, 2 + sum(e.astype(jnp.int32) for e in ends))
+    ends = [x > 0, x < nx - 1]
+    pl.semaphore_wait(barrier, nz + 1 + sum(e.astype(jnp.int32) for e in ends))
 
     def remote(ref, send, recv, device):
         return pltpu.make_async_remote_copy(
@@ -114,6 +113,18 @@
         def _():
             go_left(k, z).start()
 
+    def give(o):
+        return pltpu.make_async_remote_copy(
+            src_ref=slots_ref.at[o], dst_ref=given.at[z], send_sem=give_send.at[o],
+            recv_sem=give_recv.at[z], device_id={"cand": o}, device_id_type=MESH,
+        )
+
+    def get(o):
+        return pltpu.make_async_remote_copy(
+            src_ref=slots_ref.at[o], dst_ref=given.at[o], send_sem=give_send.at[o],
+            recv_sem=give_recv.at[o], device_id={"cand": o}, device_id_type=MESH,
+        )
+
     def x_go_right(o):
         return remote(xbuf.at[2 * o + c], x_right.at[o], x_line.at[o], {"tensor": t + 2})
 
@@ -126,6 +137,11 @@
     def x_from_pair(o):
         return remote(xbuf.at[2 * o + 1 - c], x_pair_send.at[o], x_pair_recv.at[o], {"tensor": 2 * x + 1 - c})
 
+    def give_one(d, carry):
+        give(lax.rem(z + d, nz)).start()
+        return carry
+
+    lax.fori_loop(1, nz, give_one, 0)
     for k in range(min(AHEAD, nchunk)):
         loads[k].wait()
         send_own(k)
@@ -235,7 +251,7 @@
 
         lax.fori_loop(0, cands, one, 0)
 
-    def compute(k):
+    def project(k):
         def take(d, carry):
             o = jnp.where(d < z, d, d + 1)
             from_pair(k, o).wait_recv()
@@ -256,12 +272,17 @@
 
         lax.fori_loop(0, rows // row_tile, tile, 0)
 
+    def units(first, last, unit):
+        def one(j, carry):
+            unit(j)
+            return carry
+
+        lax.fori_loop(first, last, one, 0)
+
+    def attend_if(k):
         @pl.when(lax.rem(k, stride) != 0)
         def _():
             attend(k)
-
-    def done(k):
-        return jnp.where(k < 2, 0, k)
 
     def step(k, carry):
         @pl.when(k + AHEAD < nchunk)
@@ -274,16 +295,36 @@
         def _():
             finish_x()
 
-        def inner(j, c2):
-            compute(j)
-            return c2
-
-        lax.fori_loop(done(k - 1), done(k), inner, 0)
-        relay(k, 2, nz)
+        @pl.when(k >= 2)
+        def _():
+            project(jnp.where(k == 2, 0, k - 1))
+
+        relay(k, 2, min(3, nz))
+
+        @pl.when(k == 2)
+        def _():
+            project(k - 1)
+
+        @pl.when(k >= 2)
+        def _():
+            attend_if(k - 1)
+
+        relay(k, 3, nz)
         return carry
 
     lax.fori_loop(0, nchunk, step, 0)
-    lax.fori_loop(nchunk - 1, nchunk, lambda j, c2: (compute(j), c2)[1], 0)
+    units(nchunk - 1, nchunk, project)
+    units(nchunk - 1, nchunk, attend_if)
+    mine_ref[...] = slots_ref[z].astype(jnp.float32)
+
+    def get_one(d, carry):
+        o = lax.rem(z + d, nz)
+        get(o).wait_recv()
+        mine_ref[...] += given[o].astype(jnp.float32)
+        give(o).wait_send()
+        return carry
+
+    lax.fori_loop(1, nz, get_one, 0)
 
     def drain(k, carry):
         def one(o, c2):
@@ -317,7 +358,7 @@
             x_go_left(o).wait_send()
 
 
-def reward_partial(nz, nt, x, wq, wkv, cache, grade):
+def reward_partial(nz, nt, x, wq, wkv, cache, grade, slots):
     cands, span, dx = x.shape
     rows = cands * span
     depth = wq.shape[0] * nz
@@ -329,9 +370,12 @@
     anywhere = pl.BlockSpec(memory_space=pl.ANY)
     return pl.pallas_call(
         functools.partial(project_kernel, nz, nt, per_group),
-        out_shape=jax.ShapeDtypeStruct((cands, span, HD), jnp.float32),
-        in_specs=[anywhere] * 4 + [pl.BlockSpec(memory_space=pltpu.VMEM)],
-        out_specs=pl.BlockSpec(memory_space=pltpu.VMEM),
+        out_shape=(
+            jax.ShapeDtypeStruct((cands, span, HD), jnp.float32),
+            jax.ShapeDtypeStruct(slots.shape[1:], jnp.float32),
+        ),
+        in_specs=[anywhere] * 4 + [pl.BlockSpec(memory_space=pltpu.VMEM)] * 2,
+        out_specs=(pl.BlockSpec(memory_space=pltpu.VMEM),) * 2,
         scratch_shapes=[
             pltpu.VMEM((nt, rows, dx), jnp.bfloat16),
             pltpu.VMEM((nchunk, depth, CW), jnp.bfloat16),
@@ -341,15 +385,72 @@
             dma((nchunk, nz)), dma((nchunk, nz)), dma((nchunk, nz)),
             dma((nchunk, nz)), dma((nchunk, nz)),
             dma((nx,)), dma((nx,)), dma((nx,)), dma((nx,)), dma((nx,)),
+            pltpu.VMEM(slots.shape, jnp.bfloat16), dma((nz,)), dma((nz,)),
         ],
         compiler_params=pltpu.CompilerParams(
             collective_id=0, has_side_effects=True, vmem_limit_bytes=67043328
         ),
-    )(x.reshape(rows, dx), wq, wkv, cache, grade.reshape(-1, HD))
+    )(x.reshape(rows, dx), wq, wkv, cache, grade.reshape(-1, HD), slots)
+
+
+def gather_kernel(nz, own_ref, out_ref, buf, send, recv):
+    z = lax.axis_index("cand")
+    barrier = pltpu.get_barrier_semaphore()
+
+    def greet(d, carry):
+        pl.semaphore_signal(
+            barrier, inc=1, device_id={"cand": lax.rem(z + d, nz)}, device_id_type=MESH
+        )
+        return carry
+
+    lax.fori_loop(1, nz, greet, 0)
+    pl.semaphore_wait(barrier, nz - 1)
+
+    def copy(o, lands):
+        return pltpu.make_async_remote_copy(
+            src_ref=own_ref, dst_ref=buf.at[lands], send_sem=send.at[o],
+            recv_sem=recv.at[lands], device_id={"cand": o}, device_id_type=MESH,
+        )
+
+    def start(d, carry):
+        copy(lax.rem(z + d, nz), z).start()
+        return carry
+
+    lax.fori_loop(1, nz, start, 0)
+    out_ref[z] = own_ref[...]
+
+    def finish(d, carry):
+        o = lax.rem(z + d, nz)
+        copy(o, o).wait_recv()
+        out_ref[o] = buf[o]
+        copy(o, z).wait_send()
+        return carry
+
+    lax.fori_loop(1, nz, finish, 0)
+
+
+def gather_slots(nz, own):
+    lanes, count, width = own.shape
+    flat = own.reshape(lanes * count, width)
+    vmem = pl.BlockSpec(memory_space=pltpu.VMEM)
+    whole = pl.pallas_call(
+        functools.partial(gather_kernel, nz),
+        out_shape=jax.ShapeDtypeStruct((nz,) + flat.shape, own.dtype),
+        in_specs=[vmem],
+        out_specs=vmem,
+        scratch_shapes=[
+            pltpu.VMEM((nz,) + flat.shape, own.dtype),
+            pltpu.SemaphoreType.DMA((nz,)), pltpu.SemaphoreType.DMA((nz,)),
+        ],
+        compiler_params=pltpu.CompilerParams(
+            collective_id=1, has_side_effects=True, vmem_limit_bytes=1 << 22
+        ),
+    )(flat)
+    return whole.reshape(nz * lanes, count, width)
 
 
 def policy(
-    cand_here, actor_stored_pairs, filled_extents, kept_responses, actor_latest_probes, actor_latest_pairs
+    nz, cand_here, actor_stored_pairs, filled_extents, kept_responses, actor_latest_probes, actor_latest_pairs
 ):
     key_scale = HD ** (-0.5)
     device_here = lax.axis_index("cand")
@@ -362,8 +463,8 @@
     causal_new = lax.broadcasted_iota(jnp.int32, (new_count, new_count), 0) >= lax.broadcasted_iota(
         jnp.int32, (new_count, new_count), 1
     )
-    both = lax.all_gather(
-        jnp.concatenate([actor_latest_probes, actor_latest_pairs], axis=2), "cand", axis=0, tiled=True
+    both = gather_slots(
+        nz, jnp.concatenate([actor_latest_probes, actor_latest_pairs], axis=2)
     )
     all_queries = both[..., : policy_heads * HD]
     all_fresh = both[..., policy_heads * HD:]
@@ -414,10 +515,7 @@
     placed = jnp.einsum(
         "cs,cx->sx", matched.astype(jnp.float32), flattened, precision=lax.Precision.HIGHEST
     )
-    return lax.psum_scatter(
-        placed.reshape(lane_number, new_count, policy_heads * HD).astype(jnp.bfloat16),
-        "cand", scatter_dimension=0, tiled=True,
-    )
+    return placed.reshape(nz, lane_number // nz * new_count, policy_heads * HD).astype(jnp.bfloat16)
 
 
 def local(
@@ -433,15 +531,16 @@
     actor_latest_probes,
     actor_latest_pairs,
 ):
-    shares = reward_partial(
+    slots = policy(
+        nz, response_latest_embeddings.shape[0], actor_stored_pairs, filled_extents, kept_responses,
+        actor_latest_probes, actor_latest_pairs,
+    )
+    shares, mine = reward_partial(
         nz, nt, response_latest_embeddings, critic_probe_projector, critic_pair_projector,
-        critic_stored_pairs, critic_grading_vector,
+        critic_stored_pairs, critic_grading_vector, slots,
     )
     token_rewards = lax.psum(jnp.sum(shares, axis=-1), "tensor")
-    slot_rows = policy(
-        response_latest_embeddings.shape[0], actor_stored_pairs, filled_extents, kept_responses,
-        actor_latest_probes, actor_latest_pairs,
-    )
+    slot_rows = mine.reshape(actor_latest_probes.shape).astype(jnp.bfloat16)
     return (token_rewards, slot_rows)
 
 

time: 313 us -> 285 us (0.911)
  blocking collectives: 40.2 us -> 6.24 us
  Pallas kernels: 256 us -> 262 us
    unnamed x1 -> x0, blocking collectives: 19.2 us -> none
    all_gather x1 -> x0, blocking collectives: 14.8 us -> none  [policy(): lax.all_gather(jnp.concatenate([actor_latest_probes, actor_latest_pairs],...]
    pallas_call x0 -> x1, Pallas kernels: none -> 7.58 us  [gather_slots(): pl.pallas_call(functools.partial(gather_kernel, nz), out_shape=jax.ShapeD...]
where the time goes in v3:
time: 285 us; the launch traced here: 284 us
  Pallas kernels  262 us (92%)
  local copies, waits for them, and re-layouts  7.83 us (3%)
  blocking collectives  6.24 us (2%)
  other arithmetic  4.77 us (2%)
    pallas_call x1, Pallas kernels, reward_partial(): pl.pallas_call(functools.partial(project_kernel, nz, nt, per_group), out_...  255 us
    pallas_call x1, Pallas kernels, gather_slots(): pl.pallas_call(functools.partial(gather_kernel, nz), out_shape=jax.ShapeD...  7.58 us
    psum x1, blocking collectives, local(): token_rewards = lax.psum(jnp.sum(shares, axis=-1), 'tensor')  6.24 us

profile of v3, /device:TPU:0, one launch (start us, length us, event | category | flops | bytes accessed | tf_op | source)
XLA Modules:
  0.0 284.4 jit_solution(992208703682408601)
XLA Ops:
  0.7 1.3 gather_fusion
  2.0 0.8 fusion.16
  2.8 0.1 iota_compare_fusion
  2.9 0.7 maximum_bitcast_fusion.own_ref
  3.7 7.6 %shard_map.113 = bf16[4,4,1536]{2,1,0:T(4,128)(2,1)S(1)} custom-call(bf16[4,1536]{1,0:T(4,128)(2,1)S(1)} %maximum_bitcast_fusion.own_ref), custom_call_target="tpu_custom_call" | custom-call | tf_op jit(solution)/shard_map/pallas_call | solution.py:436
  11.3 0.6 gather_fusion.1
  11.9 0.6 gather_fusion.2
  12.4 0.1 broadcast_select_fusion
  12.5 0.3 fusion.25
  12.9 4.7 %fusion.23 = (bf16[2,2048,2,128]{3,2,1,0:T(2,128)(2,1)S(1)}, bf16[2,2048,2,128]{3,2,1,0:T(2,128)(2,1)S(1)}) fusion(bf16[2,2048,2,256]{3,2,1,0:T(2,128)(2,1)} %param.15), kind=kLoop, calls=%fused_computation.54 | loop fusion | bytes 8388608 | tf_op jit(solution)/shard_map/slice | solution.py:487
  17.6 0.8 fusion.24
  18.4 0.0 copy-start
  18.4 0.6 fusion.2
  19.0 0.4 fusion.7
  19.4 0.1 fusion.11
  19.5 0.3 fusion.4
  19.9 0.0 copy-done
  19.9 0.3 fusion.15
  20.2 0.6 copy.57.slots_ref
  20.8 254.9 %shard_map.114 = (f32[2,384,128]{2,1,0:T(8,128)}, f32[4,1024]{1,0:T(4,128)}) custom-call(bf16[768,2048]{1,0:T(8,128)(2,1)} %bitcast.56, bf16[2048,1024]{1,0:T(8,128)(2,1)} %wq_ref.1, bf16[2048,512]{1,0:T(8,128)(2,1)} %wkv_ref.1, bf16[2,2048,512]{2,1,0:T(8,128)(2,1)} %cache_ref.1, f32[8,128]{1,0:T(8,128)} %bitcast.59, bf16[4,4,1024]{2,1,0:T(4,128)(2,1)} %copy.57.slots_ref), custom_call_target="tpu_custom_call" | custom-call | tf_op jit(solution)/shard_map/pallas_call | solution.py:371
  275.7 1.2 reduce_sum.42
  276.9 6.2 %psum.7 = f32[2,384]{1,0:T(2,128)} all-reduce(f32[2,384]{1,0:T(2,128)S(1)} %reduce_sum.42), channel_id=1, replica_groups=mesh['groups'=2,'cand'=4,'tensor'=4] {'tensor'}, use_global_device_ids=true, to_apply=%region_6.7 | all-reduce | flops 768 | bytes 6144 | tf_op jit(solution)/shard_map/psum | solution.py:542
  283.1 1.3 convert_bitcast_fusion
  (14 shorter events, 0.1 us)
Async XLA Ops:
  18.4 1.5 copy-start
